TPU v7x, 256 devices: a whole 4x4x8 slice. The times are simulated.
256 devices in a mesh: site: 2 (over core), wide: 32 (over x, z), narrow: 4 (over y).
Axes of the slice: x: 4, y: 4, z: 8, core: 2. Of those that a mesh axis runs over, the one named last changes fastest.
Arguments:
- initial_rows: float32 [64, 4, 2048], P('site', 'narrow'), may hold values from -6 to 6
- outcomes: int32 [64, 4], replicated, may hold values 0 or 1
- tensors: float32 [4, 2, 4, 2048, 8192], P('site', None, 'narrow', None, 'wide'), may hold values from -0.25 to 0.25
Outputs:
- final_rows: float32 [64, 4, 2048], P('site', 'narrow')
- log_weight: float32 [64], P('site')
All inputs are finite; a program needn't handle non-finite values.
Results may differ from a plain program's by a relative error of at most 0.0003.
Values sent between devices are 32-bit elements; how exact they have to be, the bound alone decides.
A program may use at most 64 MiB of HBM per device.

v0:
```python
import jax
import jax.numpy as jnp
from jax import lax
from jax.sharding import PartitionSpec as P

BOND = 8192
epsilon = 1e-06
highest = lax.Precision.HIGHEST


def from_partner(value, axis, distance):
    mask = 2**distance
    pairs = [(source, source ^ mask) for source in range(lax.axis_size(axis))]
    return lax.ppermute(value, axis, pairs)


def advance(held, log_sum, site_tensor, chosen):
    front = held.shape[0]
    groups = lax.axis_size("narrow")
    share = front // groups
    summed = lax.psum_scatter(
        jnp.einsum(
            "bar,oard->bod",
            held,
            site_tensor,
            precision=highest,
            preferred_element_type=jnp.float32,
        ),
        "narrow",
        scatter_dimension=0,
        tiled=True,
    )
    local_choice = lax.dynamic_slice_in_dim(chosen, lax.axis_index("narrow") * share, share, 0)
    squares = jnp.sum(summed * summed, axis=2)
    raw_kept = jnp.where(local_choice[:, None] == 0, summed[:, 0, :], summed[:, 1, :])
    totals = lax.psum(squares, "wide")
    both_mean = (totals[:, 0] + totals[:, 1]) / (2.0 * BOND)
    scale = lax.rsqrt(both_mean + epsilon)
    full_rows = lax.all_gather(raw_kept * scale[:, None], "wide", axis=1, tiled=True)
    kept_square = jnp.where(local_choice == 0, totals[:, 0], totals[:, 1])
    local_ratio = jnp.log(kept_square / BOND + epsilon) - jnp.log(both_mean + epsilon)
    ratio_table = jnp.broadcast_to(local_ratio[:, None], (share, groups))
    split_rows = full_rows.reshape(share, groups, -1)
    moved, moved_ratio = (
        lax.all_to_all(split_rows, "narrow", split_axis=1, concat_axis=0, tiled=True),
        lax.all_to_all(ratio_table, "narrow", split_axis=1, concat_axis=0, tiled=True),
    )
    return (moved, log_sum + moved_ratio[:, 0])


def run_section(held, log_sum, tensors, chosen_block):
    for local_site in range(tensors.shape[0]):
        held, log_sum = advance(held, log_sum, tensors[local_site], chosen_block[:, local_site])
    return (held, log_sum)


def hand_over(held, log_sum):
    moved_rows, moved_sum = from_partner((held, log_sum), "site", 0)
    return (moved_rows, moved_sum)


def shards(initial_rows, outcomes, tensors):
    section = lax.axis_index("site")
    front = initial_rows.shape[0]
    local_count = tensors.shape[0]
    section_columns = lax.dynamic_slice_in_dim(outcomes, section * local_count, local_count, 1)
    held = initial_rows
    log_sum = jnp.zeros((front,), jnp.float32)
    front_order = (section, 1 - section, section)
    for turn_index in range(3):
        new_rows, new_sum = run_section(
            held,
            log_sum,
            tensors,
            lax.dynamic_slice_in_dim(section_columns, front_order[turn_index] * front, front, 0),
        )
        if turn_index == 1:
            held, log_sum = (new_rows, new_sum)
        else:
            active = section == 0 if turn_index == 0 else section == 1
            held = jnp.where(active, new_rows, held)
            log_sum = jnp.where(active, new_sum, log_sum)
        if turn_index < 2:
            held, log_sum = hand_over(held, log_sum)
    return (held, log_sum)


def solution(mesh):
    placed = (P("site", "narrow", None), P(), P("site", None, "narrow", None, "wide"))
    return jax.shard_map(
        shards,
        mesh=mesh,
        in_specs=placed,
        out_specs=(P("site", "narrow", None), P("site")),
        check_vma=False,
    )
```

profile of v0, /device:TPU:2, one launch (start us, length us, event | category | flops | bytes accessed | tf_op | source)
XLA Modules:
  0.0 993.4 jit_solution(1777501969221541964)
XLA Ops:
  7.2 5.4 fusion.2
  12.7 0.8 fusion.33
  13.6 25.4 %reduce-scatter.7.cloned.1.call-done = f32[8,2,256]{2,0,1:T(8,128)} async-done(((f32[32,2,256]{2,0,1:T(8,128)}), f32[8,2,256]{2,0,1:T(8,128)}) %reduce-scatter.7.cloned.1.call-update) | async-done | bytes 16400 | tf_op jit(solution)/shard_map/reduce_scatter | solution.py:21
  39.0 0.8 multiply_reduce_fusion.5
  39.8 63.2 %psum.42 = f32[8,2]{0,1:T(2,128)S(1)} all-reduce(f32[8,2]{0,1:T(2,128)S(1)} %multiply_reduce_fusion.5), channel_id=1, replica_groups=mesh['site'=2,'wide'=32,'narrow'=4] {'wide'}, use_global_device_ids=true, to_apply=%region_2.3 | all-reduce | flops 16 | bytes 128 | tf_op jit(solution)/shard_map/psum | solution.py:36
  103.9 58.4 %all_gather.18 = f32[8,8192]{1,0:T(8,128)S(1)} all-gather(f32[8,256]{1,0:T(8,128)S(1)} %fusion.24), channel_id=1, replica_groups=mesh['site'=2,'wide'=32,'narrow'=4] {'wide'}, dimensions={1}, use_global_device_ids=true | all-gather | bytes 270336 | tf_op jit(solution)/shard_map/all_gather | solution.py:39
  162.3 9.2 all_to_all.171
  171.5 5.3 fusion.5
  176.9 18.2 %reduce-scatter.9.cloned.1.call-done = f32[8,2,256]{2,0,1:T(8,128)} async-done(((f32[32,2,256]{2,0,1:T(8,128)}), f32[8,2,256]{2,0,1:T(8,128)}) %reduce-scatter.9.cloned.1.call-update) | async-done | bytes 16400 | tf_op jit(solution)/shard_map/reduce_scatter | solution.py:21
  195.0 0.8 multiply_reduce_fusion.4
  195.9 63.2 %psum.43 = f32[8,2]{0,1:T(2,128)S(1)} all-reduce(f32[8,2]{0,1:T(2,128)S(1)} %multiply_reduce_fusion.4), channel_id=1, replica_groups=mesh['site'=2,'wide'=32,'narrow'=4] {'wide'}, use_global_device_ids=true, to_apply=%region_5.6 | all-reduce | flops 16 | bytes 128 | tf_op jit(solution)/shard_map/psum | solution.py:36
  260.0 62.4 %all_gather.19 = f32[8,8192]{1,0:T(8,128)} all-gather(f32[8,256]{1,0:T(8,128)S(1)} %fusion.22), channel_id=1, replica_groups=mesh['site'=2,'wide'=32,'narrow'=4] {'wide'}, dimensions={1}, use_global_device_ids=true | all-gather | bytes 270336 | tf_op jit(solution)/shard_map/all_gather | solution.py:39
  322.4 3.4 all-to-all-start.1
  325.9 6.6 all-to-all-done.1
  332.7 1.5 collective-permute-done
  334.2 5.3 fusion.1
  339.6 18.2 %reduce-scatter.11.cloned.1.call-done = f32[8,2,256]{2,0,1:T(8,128)} async-done(((f32[32,2,256]{2,0,1:T(8,128)}), f32[8,2,256]{2,0,1:T(8,128)}) %reduce-scatter.11.cloned.1.call-update) | async-done | bytes 16400 | tf_op jit(solution)/shard_map/reduce_scatter | solution.py:21
  357.8 0.8 multiply_reduce_fusion.3
  358.6 63.2 %psum.44 = f32[8,2]{0,1:T(2,128)S(1)} all-reduce(f32[8,2]{0,1:T(2,128)S(1)} %multiply_reduce_fusion.3), channel_id=1, replica_groups=mesh['site'=2,'wide'=32,'narrow'=4] {'wide'}, use_global_device_ids=true, to_apply=%region_8.9 | all-reduce | flops 16 | bytes 128 | tf_op jit(solution)/shard_map/psum | solution.py:36
  422.8 58.4 %all_gather.20 = f32[8,8192]{1,0:T(8,128)S(1)} all-gather(f32[8,256]{1,0:T(8,128)S(1)} %fusion.20), channel_id=1, replica_groups=mesh['site'=2,'wide'=32,'narrow'=4] {'wide'}, dimensions={1}, use_global_device_ids=true | all-gather | bytes 270336 | tf_op jit(solution)/shard_map/all_gather | solution.py:39
  481.1 9.2 all_to_all.172
  490.3 5.3 fusion.4
  495.7 18.1 %reduce-scatter.13.cloned.1.call-done = f32[8,2,256]{2,0,1:T(8,128)} async-done(((f32[32,2,256]{2,0,1:T(8,128)}), f32[8,2,256]{2,0,1:T(8,128)}) %reduce-scatter.13.cloned.1.call-update) | async-done | bytes 16400 | tf_op jit(solution)/shard_map/reduce_scatter | solution.py:21
  514.7 63.2 %psum.45 = f32[8,2]{0,1:T(2,128)S(1)} all-reduce(f32[8,2]{0,1:T(2,128)S(1)} %multiply_reduce_fusion.2), channel_id=1, replica_groups=mesh['site'=2,'wide'=32,'narrow'=4] {'wide'}, use_global_device_ids=true, to_apply=%region_11.12 | all-reduce | flops 16 | bytes 128 | tf_op jit(solution)/shard_map/psum | solution.py:36
  578.8 58.4 %all_gather.21 = f32[8,8192]{1,0:T(8,128)S(1)} all-gather(f32[8,256]{1,0:T(8,128)S(1)} %fusion.18), channel_id=1, replica_groups=mesh['site'=2,'wide'=32,'narrow'=4] {'wide'}, dimensions={1}, use_global_device_ids=true | all-gather | bytes 270336 | tf_op jit(solution)/shard_map/all_gather | solution.py:39
  637.2 9.2 all_to_all.173
  646.4 1.5 collective-permute-done.1
  647.9 5.3 fusion
  653.3 7.6 all_to_all.174
  661.5 3.2 all-to-all-start.7
  664.6 5.2 all-to-all-done.7
  670.0 1.4 reduce-scatter.15.cloned.1.call-done
  672.8 3.2 all-to-all-start.8
  676.0 63.3 %psum.46 = f32[8,2]{0,1:T(2,128)S(1)} all-reduce(f32[8,2]{0,1:T(2,128)S(1)} %multiply_reduce_fusion.1), channel_id=1, replica_groups=mesh['site'=2,'wide'=32,'narrow'=4] {'wide'}, use_global_device_ids=true, to_apply=%region_14.15 | all-reduce | flops 16 | bytes 128 | tf_op jit(solution)/shard_map/psum | solution.py:36
  740.7 4.7 all-to-all-start.9
  745.5 62.4 %all_gather.22 = f32[8,8192]{1,0:T(8,128)} all-gather(f32[8,256]{1,0:T(8,128)S(1)} %fusion.16), channel_id=1, replica_groups=mesh['site'=2,'wide'=32,'narrow'=4] {'wide'}, dimensions={1}, use_global_device_ids=true | all-gather | bytes 270336 | tf_op jit(solution)/shard_map/all_gather | solution.py:39
  807.9 4.8 all-to-all-start.4
  812.9 6.5 all-to-all-done.4
  819.4 5.3 fusion.3
  825.3 3.2 all-to-all-start.10
  828.6 5.1 all-to-all-done.10
  833.7 9.2 reduce-scatter.17.cloned.1.call-done
  843.8 63.2 %psum.47 = f32[8,2]{0,1:T(2,128)S(1)} all-reduce(f32[8,2]{0,1:T(2,128)S(1)} %multiply_reduce_fusion), channel_id=1, replica_groups=mesh['site'=2,'wide'=32,'narrow'=4] {'wide'}, use_global_device_ids=true, to_apply=%region_17.18 | all-reduce | flops 16 | bytes 128 | tf_op jit(solution)/shard_map/psum | solution.py:36
  907.7 3.2 all-to-all-start.11
  911.7 62.4 %all_gather.23 = f32[8,8192]{1,0:T(8,128)} all-gather(f32[8,256]{1,0:T(8,128)S(1)} %fusion.14), channel_id=1, replica_groups=mesh['site'=2,'wide'=32,'narrow'=4] {'wide'}, dimensions={1}, use_global_device_ids=true | all-gather | bytes 270336 | tf_op jit(solution)/shard_map/all_gather | solution.py:39
  974.1 4.8 all-to-all-start.5
  979.5 6.1 all-to-all-done.5
  985.6 1.0 copy.12
  (64 shorter events, 12.6 us)
Async XLA Ops:
  7.2 325.3 %copy-start = (f32[32,1,2048]{2,1,0:T(1,128)S(1)}, f32[32,1,2048]{2,1,0:T(1,128)}, u32[]{:S(2)}) copy-start(f32[32,1,2048]{2,1,0:T(1,128)} %param.3) | copy-start | bytes 786436
  7.2 31.8 %reduce-scatter.7.cloned.1.call-start = ((), (), s32[]{:S(2)}) async-start(), calls=%async_computation.18 | async-start | bytes 81920 | tf_op jit(solution)/shard_map/reduce_scatter | solution.py:21
  12.7 182.3 %reduce-scatter.9.cloned.1.call-start = ((), (), s32[]{:S(2)}) async-start(), calls=%async_computation.19 | async-start | bytes 81920 | tf_op jit(solution)/shard_map/reduce_scatter | solution.py:21
  322.4 10.1 %all-to-all-start.1 = ((f32[8,4,2048]{2,0,1:T(8,128)}), f32[8,4,2048]{2,0,1:T(8,128)S(1)}, u32[]{:S(2)}, u32[]{:S(2)}) async-start(f32[8,4,2048]{2,0,1:T(8,128)} %bitcast.19), calls=%async_computation.3 | async-start | bytes 524288 | tf_op jit(solution)/shard_map/all_to_all | solution.py:45
  325.8 31.9 %reduce-scatter.11.cloned.1.call-start = ((), (), s32[]{:S(2)}) async-start(), calls=%async_computation.20 | async-start | bytes 81920 | tf_op jit(solution)/shard_map/reduce_scatter | solution.py:21
  332.6 1.6 collective-permute-start
  339.5 174.3 %reduce-scatter.13.cloned.1.call-start = ((), (), s32[]{:S(2)}) async-start(), calls=%async_computation.21 | async-start | bytes 81920 | tf_op jit(solution)/shard_map/reduce_scatter | solution.py:21
  495.6 175.8 %reduce-scatter.15.cloned.1.call-start = ((), (), s32[]{:S(2)}) async-start(), calls=%async_computation.22 | async-start | bytes 81920 | tf_op jit(solution)/shard_map/reduce_scatter | solution.py:21
  646.4 1.5 collective-permute-start.1
  661.5 8.4 all-to-all-start.7
  670.0 154.7 %collective-permute-start.2 = (f32[32]{0:T(128)S(1)}, f32[32]{0:T(128)S(1)}, u32[]{:S(2)}, u32[]{:S(2)}) collective-permute-start(f32[32]{0:T(128)S(1)} %select_n.125), channel_id=1, source_target_pairs={{0,128},{128,0},{1,129},{129,1},{2,130},{130,2},{3,131},{131,3},{4... | collective-permute-start | bytes 392 | tf_op jit(solution)/shard_map/ppermute | solution.py:14
  672.8 67.4 %all-to-all-start.8 = ((f32[8,4,1]{0,2,1:T(1,128)}), f32[8,4,1]{0,2,1:T(1,128)S(1)}, u32[]{:S(2)}, u32[]{:S(2)}) async-start(f32[8,4,1]{0,2,1:T(1,128)} %broadcast_in_dim.99), calls=%async_computation.14 | async-start | bytes 4096 | tf_op jit(solution)/shard_map/all_to_all | solution.py:46
  740.7 67.1 %all-to-all-start.9 = ((f32[8,4,1]{0,2,1:T(1,128)}), f32[8,4,1]{0,2,1:T(1,128)S(1)}, u32[]{:S(2)}, u32[]{:S(2)}) async-start(f32[8,4,1]{0,2,1:T(1,128)} %broadcast_in_dim.100), calls=%async_computation.15 | async-start | bytes 4096 | tf_op jit(solution)/shard_map/all_to_all | solution.py:46
  807.9 11.5 %all-to-all-start.4 = ((f32[8,4,2048]{2,0,1:T(8,128)}), f32[8,4,2048]{2,0,1:T(8,128)S(1)}, u32[]{:S(2)}, u32[]{:S(2)}) async-start(f32[8,4,2048]{2,0,1:T(8,128)} %bitcast.45), calls=%async_computation.9 | async-start | bytes 524288 | tf_op jit(solution)/shard_map/all_to_all | solution.py:45
  812.7 30.3 %reduce-scatter.17.cloned.1.call-start = ((), (), s32[]{:S(2)}) async-start(), calls=%async_computation.23 | async-start | bytes 81920 | tf_op jit(solution)/shard_map/reduce_scatter | solution.py:21
  825.3 8.4 all-to-all-start.10
  828.5 150.6 %collective-permute-start.3 = (f32[32]{0:T(128)S(1)}, f32[32]{0:T(128)S(1)}, u32[]{:S(2)}, u32[]{:S(2)}) collective-permute-start(f32[32]{0:T(128)S(1)} %add_add_fusion), channel_id=1, source_target_pairs={{0,128},{128,0},{1,129},{129,1},{2,130},{130,2},{3,131},{131,3},{4... | collective-permute-start | bytes 392 | tf_op jit(solution)/shard_map/ppermute | solution.py:14
  907.7 66.4 %all-to-all-start.11 = ((f32[8,4,1]{0,2,1:T(1,128)}), f32[8,4,1]{0,2,1:T(1,128)S(1)}, u32[]{:S(2)}, u32[]{:S(2)}) async-start(f32[8,4,1]{0,2,1:T(1,128)} %broadcast_in_dim.102), calls=%async_computation.17 | async-start | bytes 4096 | tf_op jit(solution)/shard_map/all_to_all | solution.py:46
  974.1 11.4 %all-to-all-start.5 = ((f32[8,4,2048]{2,0,1:T(8,128)}), f32[8,4,2048]{2,0,1:T(8,128)S(1)}, u32[]{:S(2)}, u32[]{:S(2)}) async-start(f32[8,4,2048]{2,0,1:T(8,128)} %bitcast.53), calls=%async_computation.11 | async-start | bytes 524288 | tf_op jit(solution)/shard_map/all_to_all | solution.py:45
Sparse Core Ops, SparseCore 0:
  12.8 26.1 reduce-scatter.6
  177.0 18.0 reduce-scatter.8
  339.6 18.0 reduce-scatter.10
  495.8 18.0 reduce-scatter.12
  653.4 18.0 reduce-scatter.14
  824.8 18.0 reduce-scatter.16
where the time goes:
time: 995 us; the launch traced here: 993 us
  blocking collectives  777 us (78%)
  waiting for transfers between devices  123 us (12%)
  matrix products  31.9 us (3%)
  starting transfers between devices  30.9 us (3%)
  between operations  14.3 us (1%)
  other arithmetic  11 us (1%)
    psum x6, blocking collectives, advance(): totals = lax.psum(squares, 'wide')  379 us
    all_gather x6, blocking collectives, advance(): lax.all_gather(raw_kept * scale[:, None], 'wide', axis=1, tiled=True)  362 us
    reduce_scatter x6, waiting for transfers between devices, advance(): lax.psum_scatter(jnp.einsum('bar,oard->bod', held, site_tensor, precision...  90.4 us
    dot_general x6, matrix products, advance(): jnp.einsum('bar,oard->bod', held, site_tensor, precision=highest, preferr...  31.9 us
    all_to_all x3, blocking collectives, advance(): lax.all_to_all(split_rows, 'narrow', split_axis=1, concat_axis=0, tiled=T...  27.6 us
  transfers between devices with their start and end apart: 18, of which 13 were waited for; matrix products, arithmetic and copies ran while one was open for 1% of the time, Pallas kernels for 0%

commit v1 on v0

--- a/solution.py
+++ b/solution.py
@@ -42,7 +42,12 @@
     ratio_table = jnp.broadcast_to(local_ratio[:, None], (share, groups))
     split_rows = full_rows.reshape(share, groups, -1)
     moved, moved_ratio = (
-        lax.all_to_all(split_rows, "narrow", split_axis=1, concat_axis=0, tiled=True),
+        jnp.concatenate(
+            lax.all_to_all(
+                jnp.stack(jnp.split(split_rows, lax.axis_size("narrow"), axis=1)), "narrow", 0, 0
+            ),
+            axis=0,
+        ),
         lax.all_to_all(ratio_table, "narrow", split_axis=1, concat_axis=0, tiled=True),
     )
     return (moved, log_sum + moved_ratio[:, 0])

time: 995 us -> 989 us (level)
  blocking collectives: 777 us -> 765 us
    all_gather x6, blocking collectives: 362 us -> 350 us  [advance(): lax.all_gather(raw_kept * scale[:, None], 'wide', axis=1, tiled=True)]
  transfers between devices with their start and end apart: 18 -> 18, of which waited for: 13 -> 14; matrix products, arithmetic and copies ran while one was open for 1% -> 2% of each run, Pallas kernels for 0% -> 0%
where the time goes in v1:
time: 989 us; the launch traced here: 987 us
  blocking collectives  765 us (77%)
  waiting for transfers between devices  127 us (13%)
  matrix products  31.9 us (3%)
  starting transfers between devices  29.5 us (3%)
  between operations  14.4 us (1%)
  other arithmetic  13.2 us (1%)
    psum x6, blocking collectives, advance(): totals = lax.psum(squares, 'wide')  379 us
    all_gather x6, blocking collectives, advance(): lax.all_gather(raw_kept * scale[:, None], 'wide', axis=1, tiled=True)  350 us
    reduce_scatter x6, waiting for transfers between devices, advance(): lax.psum_scatter(jnp.einsum('bar,oard->bod', held, site_tensor, precision...  90.3 us
    dot_general x6, matrix products, advance(): jnp.einsum('bar,oard->bod', held, site_tensor, precision=highest, preferr...  31.9 us
    all_to_all x3, blocking collectives, advance(): lax.all_to_all(jnp.stack(jnp.split(split_rows, lax.axis_size('narrow'), a...  27.6 us
  transfers between devices with their start and end apart: 18, of which 14 were waited for; matrix products, arithmetic and copies ran while one was open for 2% of the time, Pallas kernels for 0%

profile of v1, /device:TPU:2, one launch (start us, length us, event | category | flops | bytes accessed | tf_op | source)
XLA Modules:
  0.0 986.6 jit_solution(17648327281878155536)
XLA Ops:
  7.2 5.4 fusion.2
  12.7 0.8 fusion.33
  13.6 25.4 %reduce-scatter.7.cloned.1.call-done = f32[8,2,256]{2,0,1:T(8,128)} async-done(((f32[32,2,256]{2,0,1:T(8,128)}), f32[8,2,256]{2,0,1:T(8,128)}) %reduce-scatter.7.cloned.1.call-update) | async-done | bytes 16400 | tf_op jit(solution)/shard_map/reduce_scatter | solution.py:21
  39.0 0.8 multiply_reduce_fusion.5
  39.8 63.2 %psum.42 = f32[8,2]{0,1:T(2,128)S(1)} all-reduce(f32[8,2]{0,1:T(2,128)S(1)} %multiply_reduce_fusion.5), channel_id=1, replica_groups=mesh['site'=2,'wide'=32,'narrow'=4] {'wide'}, use_global_device_ids=true, to_apply=%region_2.3 | all-reduce | flops 16 | bytes 128 | tf_op jit(solution)/shard_map/psum | solution.py:36
  103.9 58.4 %all_gather.18 = f32[8,8192]{1,0:T(8,128)S(1)} all-gather(f32[8,256]{1,0:T(8,128)S(1)} %fusion.24), channel_id=1, replica_groups=mesh['site'=2,'wide'=32,'narrow'=4] {'wide'}, dimensions={1}, use_global_device_ids=true | all-gather | bytes 270336 | tf_op jit(solution)/shard_map/all_gather | solution.py:39
  162.4 9.2 all_to_all.102
  171.6 5.3 fusion.5
  176.9 18.2 %reduce-scatter.9.cloned.1.call-done = f32[8,2,256]{2,0,1:T(8,128)} async-done(((f32[32,2,256]{2,0,1:T(8,128)}), f32[8,2,256]{2,0,1:T(8,128)}) %reduce-scatter.9.cloned.1.call-update) | async-done | bytes 16400 | tf_op jit(solution)/shard_map/reduce_scatter | solution.py:21
  195.1 0.8 multiply_reduce_fusion.4
  196.0 63.2 %psum.43 = f32[8,2]{0,1:T(2,128)S(1)} all-reduce(f32[8,2]{0,1:T(2,128)S(1)} %multiply_reduce_fusion.4), channel_id=1, replica_groups=mesh['site'=2,'wide'=32,'narrow'=4] {'wide'}, use_global_device_ids=true, to_apply=%region_5.6 | all-reduce | flops 16 | bytes 128 | tf_op jit(solution)/shard_map/psum | solution.py:36
  260.1 58.4 %all_gather.19 = f32[8,8192]{1,0:T(8,128)S(1)} all-gather(f32[8,256]{1,0:T(8,128)S(1)} %fusion.22), channel_id=1, replica_groups=mesh['site'=2,'wide'=32,'narrow'=4] {'wide'}, dimensions={1}, use_global_device_ids=true | all-gather | bytes 270336 | tf_op jit(solution)/shard_map/all_gather | solution.py:39
  319.2 3.4 all-to-all-start.1
  322.7 6.6 all-to-all-done.1
  329.5 1.5 collective-permute-done
  331.0 5.3 fusion.1
  336.4 18.1 %reduce-scatter.11.cloned.1.call-done = f32[8,2,256]{2,0,1:T(8,128)} async-done(((f32[32,2,256]{2,0,1:T(8,128)}), f32[8,2,256]{2,0,1:T(8,128)}) %reduce-scatter.11.cloned.1.call-update) | async-done | bytes 16400 | tf_op jit(solution)/shard_map/reduce_scatter | solution.py:21
  355.3 63.2 %psum.44 = f32[8,2]{0,1:T(2,128)S(1)} all-reduce(f32[8,2]{0,1:T(2,128)S(1)} %multiply_reduce_fusion.3), channel_id=1, replica_groups=mesh['site'=2,'wide'=32,'narrow'=4] {'wide'}, use_global_device_ids=true, to_apply=%region_8.9 | all-reduce | flops 16 | bytes 128 | tf_op jit(solution)/shard_map/psum | solution.py:36
  419.4 58.4 %all_gather.20 = f32[8,8192]{1,0:T(8,128)S(1)} all-gather(f32[8,256]{1,0:T(8,128)S(1)} %fusion.20), channel_id=1, replica_groups=mesh['site'=2,'wide'=32,'narrow'=4] {'wide'}, dimensions={1}, use_global_device_ids=true | all-gather | bytes 270336 | tf_op jit(solution)/shard_map/all_gather | solution.py:39
  477.9 9.2 all_to_all.103
  487.1 5.3 fusion.4
  492.5 18.1 %reduce-scatter.13.cloned.1.call-done = f32[8,2,256]{2,0,1:T(8,128)} async-done(((f32[32,2,256]{2,0,1:T(8,128)}), f32[8,2,256]{2,0,1:T(8,128)}) %reduce-scatter.13.cloned.1.call-update) | async-done | bytes 16400 | tf_op jit(solution)/shard_map/reduce_scatter | solution.py:21
  511.5 63.2 %psum.45 = f32[8,2]{0,1:T(2,128)S(1)} all-reduce(f32[8,2]{0,1:T(2,128)S(1)} %multiply_reduce_fusion.2), channel_id=1, replica_groups=mesh['site'=2,'wide'=32,'narrow'=4] {'wide'}, use_global_device_ids=true, to_apply=%region_11.12 | all-reduce | flops 16 | bytes 128 | tf_op jit(solution)/shard_map/psum | solution.py:36
  575.6 58.4 %all_gather.21 = f32[8,8192]{1,0:T(8,128)S(1)} all-gather(f32[8,256]{1,0:T(8,128)S(1)} %fusion.18), channel_id=1, replica_groups=mesh['site'=2,'wide'=32,'narrow'=4] {'wide'}, dimensions={1}, use_global_device_ids=true | all-gather | bytes 270336 | tf_op jit(solution)/shard_map/all_gather | solution.py:39
  634.0 9.2 all_to_all.104
  643.2 1.5 collective-permute-done.1
  644.7 5.3 fusion
  650.1 7.6 all_to_all.105
  658.3 3.2 all-to-all-start.7
  661.4 5.2 all-to-all-done.7
  666.8 1.4 reduce-scatter.15.cloned.1.call-done
  669.6 3.2 all-to-all-start.8
  672.8 63.3 %psum.46 = f32[8,2]{0,1:T(2,128)S(1)} all-reduce(f32[8,2]{0,1:T(2,128)S(1)} %multiply_reduce_fusion.1), channel_id=1, replica_groups=mesh['site'=2,'wide'=32,'narrow'=4] {'wide'}, use_global_device_ids=true, to_apply=%region_14.15 | all-reduce | flops 16 | bytes 128 | tf_op jit(solution)/shard_map/psum | solution.py:36
  737.0 58.4 %all_gather.22 = f32[8,8192]{1,0:T(8,128)S(1)} all-gather(f32[8,256]{1,0:T(8,128)S(1)} %fusion.16), channel_id=1, replica_groups=mesh['site'=2,'wide'=32,'narrow'=4] {'wide'}, dimensions={1}, use_global_device_ids=true | all-gather | bytes 270336 | tf_op jit(solution)/shard_map/all_gather | solution.py:39
  796.0 4.7 all-to-all-start.9
  801.4 4.4 all-to-all-done.9
  805.8 3.4 all-to-all-start.4
  809.5 6.4 all-to-all-done.4
  815.9 5.3 fusion.3
  821.8 3.2 all-to-all-start.10
  825.1 5.1 all-to-all-done.10
  830.3 9.1 reduce-scatter.17.cloned.1.call-done
  840.3 63.2 %psum.47 = f32[8,2]{0,1:T(2,128)S(1)} all-reduce(f32[8,2]{0,1:T(2,128)S(1)} %multiply_reduce_fusion), channel_id=1, replica_groups=mesh['site'=2,'wide'=32,'narrow'=4] {'wide'}, use_global_device_ids=true, to_apply=%region_17.18 | all-reduce | flops 16 | bytes 128 | tf_op jit(solution)/shard_map/psum | solution.py:36
  904.2 3.2 all-to-all-start.11
  908.1 58.4 %all_gather.23 = f32[8,8192]{1,0:T(8,128)S(1)} all-gather(f32[8,256]{1,0:T(8,128)S(1)} %fusion.14), channel_id=1, replica_groups=mesh['site'=2,'wide'=32,'narrow'=4] {'wide'}, dimensions={1}, use_global_device_ids=true | all-gather | bytes 270336 | tf_op jit(solution)/shard_map/all_gather | solution.py:39
  967.3 4.8 all-to-all-start.5
  972.7 6.1 all-to-all-done.5
  978.7 1.0 copy.12
  (76 shorter events, 15.8 us)
Async XLA Ops:
  7.2 322.1 %copy-start = (f32[32,1,2048]{2,1,0:T(1,128)S(1)}, f32[32,1,2048]{2,1,0:T(1,128)}, u32[]{:S(2)}) copy-start(f32[32,1,2048]{2,1,0:T(1,128)} %param.3) | copy-start | bytes 786436
  7.2 31.8 %reduce-scatter.7.cloned.1.call-start = ((), (), s32[]{:S(2)}) async-start(), calls=%async_computation.18 | async-start | bytes 81920 | tf_op jit(solution)/shard_map/reduce_scatter | solution.py:21
  12.7 182.4 %reduce-scatter.9.cloned.1.call-start = ((), (), s32[]{:S(2)}) async-start(), calls=%async_computation.19 | async-start | bytes 81920 | tf_op jit(solution)/shard_map/reduce_scatter | solution.py:21
  319.2 10.1 %all-to-all-start.1 = ((f32[4,8,1,2048]{3,1,2,0:T(8,128)}), f32[4,8,1,2048]{3,1,2,0:T(8,128)S(1)}, u32[]{:S(2)}, u32[]{:S(2)}) async-start(f32[4,8,1,2048]{3,1,2,0:T(8,128)} %pad_maximum_fusion.1), calls=%async_computation.3 | async-start | bytes 524288 | tf_op jit(solution)/shard_map/all_to_all | solution.py:46
  322.6 31.9 %reduce-scatter.11.cloned.1.call-start = ((), (), s32[]{:S(2)}) async-start(), calls=%async_computation.20 | async-start | bytes 81920 | tf_op jit(solution)/shard_map/reduce_scatter | solution.py:21
  329.4 1.6 collective-permute-start
  336.3 174.3 %reduce-scatter.13.cloned.1.call-start = ((), (), s32[]{:S(2)}) async-start(), calls=%async_computation.21 | async-start | bytes 81920 | tf_op jit(solution)/shard_map/reduce_scatter | solution.py:21
  492.4 175.8 %reduce-scatter.15.cloned.1.call-start = ((), (), s32[]{:S(2)}) async-start(), calls=%async_computation.22 | async-start | bytes 81920 | tf_op jit(solution)/shard_map/reduce_scatter | solution.py:21
  643.2 1.5 collective-permute-start.1
  658.3 8.4 all-to-all-start.7
  666.8 154.4 %collective-permute-start.2 = (f32[32]{0:T(128)S(1)}, f32[32]{0:T(128)S(1)}, u32[]{:S(2)}, u32[]{:S(2)}) collective-permute-start(f32[32]{0:T(128)S(1)} %select_n.125), channel_id=1, source_target_pairs={{0,128},{128,0},{1,129},{129,1},{2,130},{130,2},{3,131},{131,3},{4... | collective-permute-start | bytes 392 | tf_op jit(solution)/shard_map/ppermute | solution.py:14
  669.6 125.8 %all-to-all-start.8 = ((f32[8,4,1]{0,2,1:T(1,128)}), f32[8,4,1]{0,2,1:T(1,128)S(1)}, u32[]{:S(2)}, u32[]{:S(2)}) async-start(f32[8,4,1]{0,2,1:T(1,128)} %broadcast_in_dim.99), calls=%async_computation.14 | async-start | bytes 4096 | tf_op jit(solution)/shard_map/all_to_all | solution.py:51
  796.0 9.9 %all-to-all-start.9 = ((f32[8,4,1]{0,2,1:T(1,128)}), f32[8,4,1]{0,2,1:T(1,128)S(1)}, u32[]{:S(2)}, u32[]{:S(2)}) async-start(f32[8,4,1]{0,2,1:T(1,128)} %broadcast_in_dim.100), calls=%async_computation.15 | async-start | bytes 4096 | tf_op jit(solution)/shard_map/all_to_all | solution.py:51
  805.8 10.1 %all-to-all-start.4 = ((f32[4,8,1,2048]{3,1,2,0:T(8,128)}), f32[4,8,1,2048]{3,1,2,0:T(8,128)S(1)}, u32[]{:S(2)}, u32[]{:S(2)}) async-start(f32[4,8,1,2048]{3,1,2,0:T(8,128)} %pad_maximum_fusion.4), calls=%async_computation.9 | async-start | bytes 524288 | tf_op jit(solution)/shard_map/all_to_all | solution.py:46
  809.3 30.1 %reduce-scatter.17.cloned.1.call-start = ((), (), s32[]{:S(2)}) async-start(), calls=%async_computation.23 | async-start | bytes 81920 | tf_op jit(solution)/shard_map/reduce_scatter | solution.py:21
  821.8 8.4 all-to-all-start.10
  825.0 147.1 %collective-permute-start.3 = (f32[32]{0:T(128)S(1)}, f32[32]{0:T(128)S(1)}, u32[]{:S(2)}, u32[]{:S(2)}) collective-permute-start(f32[32]{0:T(128)S(1)} %add_add_fusion), channel_id=1, source_target_pairs={{0,128},{128,0},{1,129},{129,1},{2,130},{130,2},{3,131},{131,3},{4... | collective-permute-start | bytes 392 | tf_op jit(solution)/shard_map/ppermute | solution.py:14
  904.2 63.1 %all-to-all-start.11 = ((f32[8,4,1]{0,2,1:T(1,128)}), f32[8,4,1]{0,2,1:T(1,128)S(1)}, u32[]{:S(2)}, u32[]{:S(2)}) async-start(f32[8,4,1]{0,2,1:T(1,128)} %broadcast_in_dim.102), calls=%async_computation.17 | async-start | bytes 4096 | tf_op jit(solution)/shard_map/all_to_all | solution.py:51
  967.3 11.4 %all-to-all-start.5 = ((f32[4,8,1,2048]{3,1,2,0:T(8,128)}), f32[4,8,1,2048]{3,1,2,0:T(8,128)S(1)}, u32[]{:S(2)}, u32[]{:S(2)}) async-start(f32[4,8,1,2048]{3,1,2,0:T(8,128)} %pad_maximum_fusion.5), calls=%async_computation.11 | async-start | bytes 524288 | tf_op jit(solution)/shard_map/all_to_all | solution.py:46
Sparse Core Ops, SparseCore 0:
  12.8 26.1 reduce-scatter.6
  177.0 18.0 reduce-scatter.8
  336.4 18.0 reduce-scatter.10
  492.5 18.0 reduce-scatter.12
  650.2 18.0 reduce-scatter.14
  821.3 18.0 reduce-scatter.16
